TPU v7x, 32 devices: a whole 2x2x4 slice. The times are simulated.
32 devices in a mesh: dp: 16 (over z, y, x), tensor: 2 (over core).
Axes of the slice: x: 2, y: 2, z: 4, core: 2. Of those that a mesh axis runs over, the one named last changes fastest.
Arguments:
- layer_in: bfloat16 [8192, 768], P(('dp', 'tensor')), may hold values from -6 to 6
- norm1_gain: bfloat16 [768], P('tensor'), may hold values from 0.5 to 1.5
- qkv_weight: bfloat16 [768, 2304], P('tensor'), may hold values from -0.21875 to 0.21875
- out_weight: bfloat16 [768, 768], P('tensor'), may hold values from -4 to 4
- norm2_gain: bfloat16 [768], P('tensor'), may hold values from 0.5 to 1.5
- mlp_weight: bfloat16 [3, 768, 1152], P(None, None, 'tensor'), may hold values from -0.21875 to 0.21875
- cotangent: bfloat16 [8192, 768], P(('dp', 'tensor')), may hold values from -6 to 6
Outputs:
- layer_out: bfloat16 [8192, 768], P(('dp', 'tensor'))
- input_grad: float32 [8192, 768], P(('dp', 'tensor'))
- norm1_grad: float32 [768], P('tensor')
- qkv_grad: float32 [768, 2304], P('tensor')
- out_grad: float32 [768, 768], P('tensor')
- norm2_grad: float32 [768], P('tensor')
- mlp_grad: float32 [3, 768, 1152], P(None, None, 'tensor')
All inputs are finite; a program needn't handle non-finite values.
Results may differ from a plain program's by a relative error of at most 0.023.
Values may be sent and summed in bfloat16 or wider, within the bound.
A program may use at most 128 MiB of HBM per device.

v0:
```python
import jax
import jax.numpy as jnp
from jax import lax
from jax.sharding import PartitionSpec as P

HEADS = 12
HEAD_DIM = 64
SEQ = 512
EPS = 1e-05
THETA = 160000.0


def swapped(value, axis, distance):
    mask = 2**distance
    pairs = [(source, source ^ mask) for source in range(lax.axis_size(axis))]
    return lax.ppermute(value, axis, pairs)


def rope_tables(positions):
    half = HEAD_DIM // 2
    freq = THETA ** (-jnp.arange(half).astype(jnp.float32) * 2.0 / HEAD_DIM)
    angle = positions.astype(jnp.float32)[:, None] * freq[None, :]
    return (jnp.cos(angle)[:, None, :], jnp.sin(angle)[:, None, :])


def rotate(values, cosine, sine):
    half = HEAD_DIM // 2
    first, second = (values[..., :half], values[..., half:])
    return jnp.concatenate([first * cosine - second * sine, second * cosine + first * sine], -1)


def unrotate(values, cosine, sine):
    half = HEAD_DIM // 2
    first, second = (values[..., :half], values[..., half:])
    return jnp.concatenate([first * cosine + second * sine, second * cosine - first * sine], -1)


def layer_norm_forward(values, gain):
    centred = values - jnp.mean(values, -1, keepdims=True)
    inverse = lax.rsqrt(jnp.mean(centred * centred, -1, keepdims=True) + EPS)
    normed = centred * inverse
    return (normed * gain, normed, inverse)


def layer_norm_backward(upstream, normed, inverse, gain):
    scaled = upstream * gain
    back = inverse * (
        scaled
        - jnp.mean(scaled, -1, keepdims=True)
        - normed * jnp.mean(scaled * normed, -1, keepdims=True)
    )
    return (back, jnp.sum(upstream * normed, 0))


def gelu_parts(values):
    cdf = 0.5 * (1.0 + jax.scipy.special.erf(values * 0.7071067811865476))
    density = jnp.exp(-0.5 * values * values) * 0.3989422804014327
    return (values * cdf, cdf + values * density)


def right_product(left, weight):
    return lax.dot_general(
        left, weight, (((1,), (1,)), ((), ())), preferred_element_type=jnp.float32
    )


def left_product(left, right):
    return lax.dot_general(
        left, right, (((0,), (0,)), ((), ())), preferred_element_type=jnp.float32
    )


def collect_keys(key_own, value_own, position_slot):
    pair = (key_own, value_own)
    far_key, far_value = swapped((pair[0], pair[1]), "tensor", 0)
    upper = (position_slot >> 0) % 2 == 1
    pair = (
        jnp.where(
            upper, jnp.concatenate([far_key, pair[0]], 0), jnp.concatenate([pair[0], far_key], 0)
        ),
        jnp.where(
            upper,
            jnp.concatenate([far_value, pair[1]], 0),
            jnp.concatenate([pair[1], far_value], 0),
        ),
    )
    return pair


def return_grads(key_grad, value_grad, position_slot):
    pair = (key_grad, value_grad)
    middle = pair[0].shape[0] // 2
    upper = (position_slot >> 0) % 2 == 1
    keep_key = jnp.where(upper, pair[0][middle:], pair[0][:middle])
    send_key = jnp.where(upper, pair[0][:middle], pair[0][middle:])
    keep_value = jnp.where(upper, pair[1][middle:], pair[1][:middle])
    send_value = jnp.where(upper, pair[1][:middle], pair[1][middle:])
    back_key = swapped(send_key.astype(jnp.bfloat16), "tensor", 0).astype(send_key.dtype)
    back_value = swapped(send_value.astype(jnp.bfloat16), "tensor", 0).astype(send_value.dtype)
    pair = (keep_key + back_key, keep_value + back_value)
    return pair


def body(layer_in, norm1_gain, qkv_weight, out_weight, norm2_gain, mlp_weight, cotangent):
    f32 = jnp.float32
    bf16 = jnp.bfloat16
    rows = layer_in.shape[0]
    width = layer_in.shape[1]
    span = SEQ // rows
    scale = HEAD_DIM ** (-0.5)
    first_norm_gain, second_norm_gain, w_qkv, w_out = (
        lax.all_gather(norm1_gain, "tensor", axis=0, tiled=True),
        lax.all_gather(norm2_gain, "tensor", axis=0, tiled=True),
        lax.all_gather(qkv_weight, "tensor", axis=0, tiled=True),
        lax.all_gather(out_weight, "tensor", axis=0, tiled=True),
    )
    first_norm_gain = first_norm_gain.astype(f32)
    second_norm_gain = second_norm_gain.astype(f32)
    position_slot = lax.axis_index("tensor") % span
    cosine, sine = rope_tables(position_slot * rows + jnp.arange(rows, dtype=jnp.int32))
    input_float_rows = layer_in.astype(f32)
    first_normed_rows, standardized_first, inverse_deviation_first = layer_norm_forward(
        input_float_rows, first_norm_gain
    )
    h1 = first_normed_rows.astype(bf16)
    qkv = jnp.dot(h1, w_qkv, preferred_element_type=f32)
    query = rotate(qkv[:, :width].reshape(rows, HEADS, HEAD_DIM), cosine, sine).astype(bf16)
    key_own = (
        rotate(qkv[:, width : 2 * width].reshape(rows, HEADS, HEAD_DIM), cosine, sine)
        .astype(bf16)
        .reshape(rows, width)
    )
    value_own = qkv[:, 2 * width :].astype(bf16)
    key_all, value_all = collect_keys(key_own, value_own, position_slot)
    keys = key_all.reshape(SEQ, HEADS, HEAD_DIM)
    values = value_all.reshape(SEQ, HEADS, HEAD_DIM)
    scores = jnp.einsum("qhd,khd->hqk", query, keys, preferred_element_type=f32) * scale
    total = jnp.log(jnp.sum(jnp.exp(scores), -1))
    probs_b = jnp.exp(scores - total[..., None]).astype(bf16)
    attended = (
        jnp.einsum("hqk,khd->qhd", probs_b, values, preferred_element_type=f32)
        .astype(bf16)
        .reshape(rows, width)
    )
    attention_mixed = input_float_rows + jnp.dot(attended, w_out, preferred_element_type=f32)
    second_normed_rows, standardized_second, inverse_deviation_second = layer_norm_forward(
        attention_mixed, second_norm_gain
    )
    h2 = second_normed_rows.astype(bf16)
    dz_f = cotangent.astype(f32)
    group = lax.all_gather(h2, "tensor", axis=0, tiled=True)
    gate_pre = jnp.dot(group, mlp_weight[0], preferred_element_type=f32)
    up_pre = jnp.dot(group, mlp_weight[1], preferred_element_type=f32)
    gel, slope = gelu_parts(gate_pre)
    hidden = (gel * up_pre).astype(bf16)
    branch = lax.psum_scatter(
        right_product(hidden, mlp_weight[2]).astype(jnp.bfloat16),
        "tensor",
        scatter_dimension=0,
        tiled=True,
    ).astype(jnp.float32)
    layer_out = (attention_mixed + branch).astype(bf16)
    grad_group = lax.all_gather(cotangent, "tensor", axis=0, tiled=True)
    grad_hidden = jnp.dot(grad_group, mlp_weight[2], preferred_element_type=f32)
    grad_gate = (grad_hidden * up_pre * slope).astype(bf16)
    grad_up = (grad_hidden * gel).astype(bf16)
    grad_mlp = jnp.stack(
        [
            left_product(group, grad_gate),
            left_product(group, grad_up),
            left_product(grad_group, hidden),
        ]
    )
    gradient_hidden_second = lax.psum_scatter(
        right_product(grad_gate, mlp_weight[0]) + right_product(grad_up, mlp_weight[1]),
        "tensor",
        scatter_dimension=0,
        tiled=True,
    )
    second_norm_backward, gradient_gain_second = layer_norm_backward(
        gradient_hidden_second, standardized_second, inverse_deviation_second, second_norm_gain
    )
    grad_mixed = dz_f + second_norm_backward
    grad_mixed_b = grad_mixed.astype(bf16)
    grad_wout = left_product(attended, grad_mixed_b)
    grad_att = right_product(grad_mixed_b, w_out).astype(bf16).reshape(rows, HEADS, HEAD_DIM)
    scores = jnp.einsum("qhd,khd->hqk", query, keys, preferred_element_type=f32) * scale
    probs = jnp.exp(scores - total[..., None])
    probs_b = probs.astype(bf16)
    grad_probs = jnp.einsum("qhd,khd->hqk", grad_att, values, preferred_element_type=f32)
    delta = jnp.einsum(
        "qhd,qhd->hq", grad_att.astype(f32), attended.reshape(rows, HEADS, HEAD_DIM).astype(f32)
    )
    grad_scores = (probs * (grad_probs - delta[..., None])).astype(bf16)
    grad_query = jnp.einsum("hqk,khd->qhd", grad_scores, keys, preferred_element_type=f32) * scale
    grad_keys = jnp.einsum("hqk,qhd->khd", grad_scores, query, preferred_element_type=f32) * scale
    grad_values = jnp.einsum("hqk,qhd->khd", probs_b, grad_att, preferred_element_type=f32)
    key_total, value_total = return_grads(
        grad_keys.reshape(SEQ, width), grad_values.reshape(SEQ, width), position_slot
    )
    grad_q = unrotate(grad_query, cosine, sine).reshape(rows, width)
    grad_k = unrotate(key_total.reshape(rows, HEADS, HEAD_DIM), cosine, sine).reshape(rows, width)
    grad_qkv = jnp.concatenate([grad_q, grad_k, value_total], 1).astype(bf16)
    grad_wqkv = left_product(h1, grad_qkv)
    gradient_hidden_first = right_product(grad_qkv, w_qkv)
    first_norm_backward, gradient_gain_first = layer_norm_backward(
        gradient_hidden_first, standardized_first, inverse_deviation_first, first_norm_gain
    )
    input_grad = grad_mixed + first_norm_backward
    shares = (
        lax.psum_scatter(
            grad_wqkv.astype(jnp.bfloat16), "tensor", scatter_dimension=0, tiled=True
        ).astype(jnp.float32),
        lax.psum_scatter(
            grad_wout.astype(jnp.bfloat16), "tensor", scatter_dimension=0, tiled=True
        ).astype(jnp.float32),
        lax.psum_scatter(
            gradient_gain_first.astype(jnp.bfloat16), "tensor", scatter_dimension=0, tiled=True
        ).astype(jnp.float32),
        lax.psum_scatter(
            gradient_gain_second.astype(jnp.bfloat16), "tensor", scatter_dimension=0, tiled=True
        ).astype(jnp.float32),
    )
    totals = (
        lax.psum(shares[0].astype(jnp.bfloat16), "dp").astype(jnp.float32),
        lax.psum(shares[1].astype(jnp.bfloat16), "dp").astype(jnp.float32),
        lax.psum(shares[2].astype(jnp.bfloat16), "dp").astype(jnp.float32),
        lax.psum(shares[3].astype(jnp.bfloat16), "dp").astype(jnp.float32),
        lax.psum(grad_mlp.astype(jnp.bfloat16), "dp").astype(jnp.float32),
    )
    return (layer_out, input_grad, totals[2], totals[0], totals[1], totals[3], totals[4])


def solution(mesh):
    return jax.shard_map(
        body,
        mesh=mesh,
        in_specs=(
            P(("dp", "tensor"), None),
            P("tensor"),
            P("tensor", None),
            P("tensor", None),
            P("tensor"),
            P(None, None, "tensor"),
            P(("dp", "tensor"), None),
        ),
        out_specs=(
            P(("dp", "tensor"), None),
            P(("dp", "tensor"), None),
            P("tensor"),
            P("tensor", None),
            P("tensor", None),
            P("tensor"),
            P(None, None, "tensor"),
        ),
        check_vma=False,
    )
```

profile of v0, /device:TPU:0, one launch (start us, length us, event | category | flops | bytes accessed | tf_op | source)
XLA Modules:
  0.0 339.7 jit_solution(17604484921782706955)
XLA Ops:
  8.8 2.0 all-gather
  11.3 1.8 all-gather.1
  14.0 11.1 %all-gather.5.cloned.1.call-done = bf16[768,2304]{1,0:T(8,128)(2,1)} async-done(((bf16[384,2304]{1,0:T(8,128)(2,1)}), bf16[768,2304]{1,0:T(8,128)(2,1)}) %all-gather.5.cloned.1.call-update) | async-done | bytes 3538960 | tf_op jit(solution)/shard_map/all_gather | solution.py:114
  25.0 3.1 fusion.89
  29.4 1.4 copy.32
  33.2 2.5 all_gather.23
  37.3 1.3 copy.29
  38.6 4.9 %fusion.71 = f32[12,256,512]{2,1,0:T(8,128)} fusion(bf16[256,12,32]{0,2,1:T(8,128)(2,1)S(1)} %get-tuple-element.32, bf16[256,12,32]{0,2,1:T(8,128)(2,1)S(1)} %get-tuple-element.31, bf16[256,12,64]{0,2,1:T(8,128)(2,1)S(1)} %maximum_convert_fusion, bf16[256,12,64]{0,2,1:T(8,128)(2,1)} %bitcast.7, pred[]{:T(512)S(6)} %eq.8), kind=kOutput, calls=%fused_computation.109 | convolution fusion | flops 205651968 | bytes 7471105 | tf_op jit(solution)/shard_map/qhd,khd->hqk/dot_general | solution.py:137
  43.6 7.0 %fusion.18 = bf16[12,64,256]{2,1,0:T(8,128)(2,1)S(1)} fusion(f32[12,256,512]{2,1,0:T(8,128)} %fusion.71, bf16[256,12,64]{0,2,1:T(8,128)(2,1)S(1)} %bitcast.91, bf16[256,12,64]{0,2,1:T(8,128)(2,1)S(1)} %bitcast.93, pred[]{:T(512)S(6)} %eq.8), kind=kOutput, calls=%fused_computation.29 | convolution fusion | flops 211357184 | bytes 7471105 | tf_op jit(solution)/shard_map/hqk,khd->qhd/dot_general | solution.py:141
  50.6 1.9 fusion.92
  52.9 2.5 all_gather.22
  59.4 2.0 convolution_add_fusion
  61.5 2.9 convolution_convert_fusion.5
  64.6 7.2 %fusion.1 = f32[12,256,512]{2,1,0:T(8,128)} fusion(bf16[256,12,32]{0,2,1:T(8,128)(2,1)S(1)} %get-tuple-element.32, bf16[256,12,32]{0,2,1:T(8,128)(2,1)S(1)} %get-tuple-element.31, bf16[256,12,64]{0,2,1:T(8,128)(2,1)S(1)} %maximum_convert_fusion, bf16[256,12,64]{0,2,1:T(8,128)(2,1)} %bitcast.7, pred[]{:T(512)S(6)} %eq.8), kind=kOutput, calls=%fused_computation.2 | convolution fusion | flops 416026112 | bytes 7471105 | tf_op jit(solution)/shard_map/reduce_sum | solution.py:138
  71.8 2.2 multiply_reduce_fusion
  74.6 9.4 %reduce-scatter.5.cloned.1.call-done = bf16[256,768]{1,0:T(8,128)(2,1)} async-done(((bf16[512,768]{1,0:T(8,128)(2,1)}), bf16[256,768]{1,0:T(8,128)(2,1)}) %reduce-scatter.5.cloned.1.call-update) | async-done | bytes 393232 | tf_op jit(solution)/shard_map/reduce_scatter | solution.py:156
  83.9 2.1 multiply_add_fusion
  86.0 1.5 convolution_convert_fusion.1
  88.6 8.0 %fusion.11 = f32[512,12,64]{0,2,1:T(8,128)} fusion(bf16[256,12,64]{0,2,1:T(8,128)(2,1)S(1)} %bitcast.84, f32[12,256,512]{2,1,0:T(8,128)} %fusion.71), kind=kOutput, calls=%fused_computation.18 | convolution fusion | flops 207621632 | bytes 8257536 | tf_op jit(solution)/shard_map/hqk,qhd->khd/dot_general | solution.py:197
  96.7 4.6 %multiply_convert_fusion = bf16[12,256,512]{2,1,0:T(8,128)(2,1)S(1)} fusion(f32[12,256,512]{2,1,0:T(8,128)} %fusion.1, f32[12,256]{1,0:T(8,128)S(1)} %fusion.59, bf16[256,12,64]{0,2,1:T(8,128)(2,1)} %bitcast.86, bf16[256,12,64]{0,2,1:T(8,128)(2,1)} %bitcast.92, bf16[256,12,64]{0,2,1:T(8,128)(2,1)} %bitcast.94, pred[]{:T(512)S(6)} %eq.8), kind=kOutput, calls=%fused_computation.3 | convolution fusion | flops 209584128 | bytes 10629121 | tf_op jit(solution)/shard_map/qhd,khd->hqk/dot_general | solution.py:190
  104.2 1.6 slice_select_fusion.1
  107.1 2.2 fusion.17
  111.7 3.1 convolution_convert_fusion
  115.9 1.7 fusion.14
  119.3 1.8 pad_maximum_fusion
  121.1 8.7 %reduce-scatter.9.cloned.1.call-done = bf16[384,2304]{1,0:T(8,128)(2,1)} async-done(((bf16[768,2304]{1,0:T(8,128)(2,1)}), bf16[384,2304]{1,0:T(8,128)(2,1)}) %reduce-scatter.9.cloned.1.call-update) | async-done | bytes 1769488 | tf_op jit(solution)/shard_map/reduce_scatter | solution.py:211
  131.7 3.4 %fusion.56 = (bf16[768]{0:T(1024)(128)(2,1)S(1)}, f32[256]{0:T(256)S(1)}, f32[256]{0:T(256)S(1)}, f32[256,768]{1,0:T(8,128)S(1)}) fusion(bf16[256,768]{1,0:T(8,128)(2,1)S(1)} %copy-done.2, f32[256]{0:T(256)S(1)} %copy-done.36, f32[256]{0:T(256)S(1)} %broadcast_multiply_fusion.5, f32[768]{0:T(1024)S(1)} %reshape.182, ...), kind=kOutput, calls=%fused_computation.64 | convolution fusion | flops 911276800 | bytes 5906944 | tf_op jit(solution)/shard_map/dot_general | solution.py:62
  135.2 2.5 all-reduce.4
  137.8 44.4 %all-reduce.2 = (bf16[384]{0:T(512)(128)(2,1)S(1)}, bf16[384]{0:T(512)(128)(2,1)S(1)}) all-reduce(bf16[384]{0:T(512)(128)(2,1)S(1)} %dynamic-slice.1, bf16[384]{0:T(512)(128)(2,1)S(1)} %dynamic-slice.3), channel_id=1, replica_groups=mesh['dp'=16,'tensor'=2] {'dp'}, use_global_device_ids=true, to_apply=%region_13.14 | all-reduce | flops 768 | bytes 3072 | tf_op jit(solution)/shard_map/psum | solution.py:227
  184.6 140.7 %all-reduce.7.cloned.1.call-done = (bf16[384,2304]{1,0:T(8,128)(2,1)}, bf16[384,768]{1,0:T(8,128)(2,1)}, bf16[3,768,576]{1,2,0:T(8,128)(2,1)}) async-done(((bf16[384,2304]{1,0:T(8,128)(2,1)}, bf16[384,768]{1,0:T(8,128)(2,1)}, bf16[3,768,576]{1,2,0:T(8,128)(2,1)}), (bf16[384,2304]{1,0:T(8,128)(2,1)}, bf16[384,768]{1,0:T(8,128)(2,1)}, bf16[3,768,576]{1,2,0:T(8,128)(2,1)})) %all-reduce.7.cloned.1.call-update) | async-done | bytes 5013520 | tf_op jit(solution)/shard_map/psum | solution.py:225
  325.3 3.6 %convert_element_type.167 = f32[384,2304]{1,0:T(8,128)} convert(bf16[384,2304]{1,0:T(8,128)(2,1)} %get-tuple-element.15) | non-fusion elementwise | flops 884736 | bytes 5308416 | tf_op jit(solution)/shard_map/convert_element_type | solution.py:225
  330.0 2.8 convert_element_type.172
  (165 shorter events, 28.5 us)
Async XLA Ops:
  7.2 3.6 %copy-start.2 = (bf16[256,768]{1,0:T(8,128)(2,1)S(1)}, bf16[256,768]{1,0:T(8,128)(2,1)}, u32[]{:S(2)}) copy-start(bf16[256,768]{1,0:T(8,128)(2,1)} %param.7) | copy-start | bytes 1179652
  7.2 4.1 %copy-start.39 = (bf16[384]{0:T(512)(128)(2,1)S(1)}, bf16[384]{0:T(512)(128)(2,1)}, u32[]{:S(2)}) copy-start(bf16[384]{0:T(512)(128)(2,1)} %param.11) | copy-start | bytes 2308
  7.2 17.8 %all-gather.5.cloned.1.call-start = ((), (), s32[]{:S(2)}) async-start(), calls=%async_computation.4 | async-start | bytes 5308416 | tf_op jit(solution)/shard_map/all_gather | solution.py:114
  7.9 42.7 %all-gather.7.cloned.1.call-start = ((), (), s32[]{:S(2)}) async-start(), calls=%async_computation.5 | async-start | bytes 1769472 | tf_op jit(solution)/shard_map/all_gather | solution.py:115
  8.7 63.1 %reduce-scatter.7.cloned.1.call-start = ((), (), s32[]{:S(2)}) async-start(), calls=%async_computation.7 | async-start | bytes 2359296 | tf_op jit(solution)/shard_map/reduce_scatter | solution.py:174
  11.2 17.0 %copy-start.35 = (f32[256]{0:T(256)}, f32[256]{0:T(256)S(1)}, u32[]{:S(2)}) copy-start(f32[256]{0:T(256)S(1)} %add_rsqrt_fusion.1) | copy-start | bytes 3076
  31.8 5.1 %copy-start.10 = (f32[256,768]{1,0:T(8,128)S(1)}, f32[256,768]{1,0:T(8,128)}, u32[]{:S(2)}) copy-start(f32[256,768]{1,0:T(8,128)} %get-tuple-element.24) | copy-start | bytes 2359300
  32.6 32.0 %copy-start.19 = (bf16[256,12,64]{0,2,1:T(8,128)(2,1)}, bf16[256,12,64]{0,2,1:T(8,128)(2,1)S(1)}, u32[]{:S(2)}) copy-start(bf16[256,12,64]{0,2,1:T(8,128)(2,1)S(1)} %maximum_convert_fusion) | copy-start | bytes 1179652
  32.6 4.6 %copy-start.28 = (f32[256,32]{0,1:T(8,128)S(1)}, f32[256,32]{0,1:T(8,128)}, u32[]{:S(2)}) copy-start(f32[256,32]{0,1:T(8,128)} %get-tuple-element.37) | copy-start | bytes 98308
  32.6 4.6 %copy-start.30 = (f32[256,32]{0,1:T(8,128)S(1)}, f32[256,32]{0,1:T(8,128)}, u32[]{:S(2)}) copy-start(f32[256,32]{0,1:T(8,128)} %get-tuple-element.38) | copy-start | bytes 98308
  32.6 6.0 %collective-permute-start.1 = (bf16[256,768]{0,1:T(8,128)(2,1)S(1)}, bf16[256,768]{0,1:T(8,128)(2,1)}, u32[]{:S(2)}, u32[]{:S(2)}) collective-permute-start(bf16[256,768]{0,1:T(8,128)(2,1)S(1)} %bitcast.90), channel_id=1, source_target_pairs={{0,1},{1,0},{2,3},{3,2},{4,5},{5,4},{6,7},{7,6},{8,9},{9,8},{10,11... | collective-permute-start | bytes 1179656 | tf_op jit(solution)/shard_map/ppermute | solution.py:16
  32.9 4.4 %collective-permute-start = (bf16[256,768]{1,0:T(8,128)(2,1)}, bf16[256,768]{1,0:T(8,128)(2,1)}, u32[]{:S(2)}, u32[]{:S(2)}) collective-permute-start(bf16[256,768]{1,0:T(8,128)(2,1)} %slice.148), channel_id=1, source_target_pairs={{0,1},{1,0},{2,3},{3,2},{4,5},{5,4},{6,7},{7,6},{8,9},{9,8},{10,11... | collective-permute-start | bytes 1179656 | tf_op jit(solution)/shard_map/ppermute | solution.py:16
  36.9 6.7 %copy-start.21 = (bf16[256,768]{0,1:T(8,128)(2,1)}, bf16[256,768]{0,1:T(8,128)(2,1)S(1)}, u32[]{:S(2)}) copy-start(bf16[256,768]{0,1:T(8,128)(2,1)S(1)} %copy.30) | copy-start | bytes 1179652
  37.3 27.3 %copy-start.13 = (bf16[256,12,32]{0,2,1:T(8,128)(2,1)}, bf16[256,12,32]{0,2,1:T(8,128)(2,1)S(1)}, u32[]{:S(2)}) copy-start(bf16[256,12,32]{0,2,1:T(8,128)(2,1)S(1)} %get-tuple-element.31) | copy-start | bytes 589828
  37.3 27.3 %copy-start.15 = (bf16[256,12,32]{0,2,1:T(8,128)(2,1)}, bf16[256,12,32]{0,2,1:T(8,128)(2,1)S(1)}, u32[]{:S(2)}) copy-start(bf16[256,12,32]{0,2,1:T(8,128)(2,1)S(1)} %get-tuple-element.32) | copy-start | bytes 589828
  38.6 5.0 %copy-start.22 = (bf16[256,768]{0,1:T(8,128)(2,1)}, bf16[256,768]{0,1:T(8,128)(2,1)S(1)}, u32[]{:S(2)}) copy-start(bf16[256,768]{0,1:T(8,128)(2,1)S(1)} %copy.29) | copy-start | bytes 1179652
  52.7 3.4 copy-start.34
  61.4 22.5 %reduce-scatter.5.cloned.1.call-start = ((), (), s32[]{:S(2)}) async-start(), calls=%async_computation.6 | async-start | bytes 1179648 | tf_op jit(solution)/shard_map/reduce_scatter | solution.py:156
  64.3 56.8 %reduce-scatter.11.cloned.1.call-start = ((), (), s32[]{:S(2)}) async-start(), calls=%async_computation.9 | async-start | bytes 1769472 | tf_op jit(solution)/shard_map/reduce_scatter | solution.py:214
  71.8 12.1 %copy-start.18 = (bf16[256,768]{1,0:T(8,128)(2,1)S(1)}, bf16[256,768]{1,0:T(8,128)(2,1)}, u32[]{:S(2)}) copy-start(bf16[256,768]{1,0:T(8,128)(2,1)} %param.13) | copy-start | bytes 1179652
  71.8 12.1 %copy-start.9 = (f32[256,768]{1,0:T(8,128)S(1)}, f32[256,768]{1,0:T(8,128)}, u32[]{:S(2)}) copy-start(f32[256,768]{1,0:T(8,128)} %reduce-scatter.7.cloned.1.call-done) | copy-start | bytes 2359300
  88.6 8.0 %copy-start.8 = (bf16[256,768]{0,1:T(8,128)(2,1)}, bf16[256,768]{0,1:T(8,128)(2,1)S(1)}, u32[]{:S(2)}) copy-start(bf16[256,768]{0,1:T(8,128)(2,1)S(1)} %copy.33) | copy-start | bytes 1179652
  96.7 4.6 %copy-start.14 = (bf16[256,12,32]{0,2,1:T(8,128)(2,1)S(1)}, bf16[256,12,32]{0,2,1:T(8,128)(2,1)}, u32[]{:S(2)}) copy-start(bf16[256,12,32]{0,2,1:T(8,128)(2,1)} %copy-done.13) | copy-start | bytes 589828
  96.7 4.6 %copy-start.16 = (bf16[256,12,32]{0,2,1:T(8,128)(2,1)S(1)}, bf16[256,12,32]{0,2,1:T(8,128)(2,1)}, u32[]{:S(2)}) copy-start(bf16[256,12,32]{0,2,1:T(8,128)(2,1)} %copy-done.15) | copy-start | bytes 589828
  104.0 5.4 %collective-permute-start.2 = (bf16[256,768]{0,1:T(8,128)(2,1)}, bf16[256,768]{0,1:T(8,128)(2,1)}, u32[]{:S(2)}, u32[]{:S(2)}) collective-permute-start(bf16[256,768]{0,1:T(8,128)(2,1)} %bitcast.21), channel_id=1, source_target_pairs={{0,1},{1,0},{2,3},{3,2},{4,5},{5,4},{6,7},{7,6},{8,9},{9,8},{10,11... | collective-permute-start | bytes 1179656 | tf_op jit(solution)/shard_map/ppermute | solution.py:16
  104.2 25.6 %reduce-scatter.9.cloned.1.call-start = ((), (), s32[]{:S(2)}) async-start(), calls=%async_computation.8 | async-start | bytes 5308416 | tf_op jit(solution)/shard_map/reduce_scatter | solution.py:211
  106.3 4.5 %collective-permute-start.3 = (bf16[256,768]{0,1:T(8,128)(2,1)S(1)}, bf16[256,768]{0,1:T(8,128)(2,1)S(1)}, u32[]{:S(2)}, u32[]{:S(2)}) collective-permute-start(bf16[256,768]{0,1:T(8,128)(2,1)S(1)} %bitcast.99), channel_id=1, source_target_pairs={{0,1},{1,0},{2,3},{3,2},{4,5},{5,4},{6,7},{7,6},{8,9},{9,8},{10,11... | collective-permute-start | bytes 1179656 | tf_op jit(solution)/shard_map/ppermute | solution.py:16
  114.8 210.4 %all-reduce.7.cloned.1.call-start = ((), (), s32[]{:S(2)}) async-start(), calls=%async_computation.10 | async-start | bytes 10027008 | tf_op jit(solution)/shard_map/psum | solution.py:225
  131.7 3.4 %copy-start.37 = (bf16[768]{0:T(1024)(128)(2,1)S(1)}, bf16[768]{0:T(1024)(128)(2,1)}, u32[]{:S(2)}) copy-start(bf16[768]{0:T(1024)(128)(2,1)} %get-tuple-element.7) | copy-start | bytes 4612
  131.7 51.7 %copy-start.1 = (f32[256,768]{1,0:T(8,128)S(1)}, f32[256,768]{1,0:T(8,128)}, u32[]{:S(2)}) copy-start(f32[256,768]{1,0:T(8,128)} %copy-done) | copy-start | bytes 2359300
  325.3 3.7 %copy-start.27 = (bf16[384,768]{1,0:T(8,128)(2,1)S(1)}, bf16[384,768]{1,0:T(8,128)(2,1)}, u32[]{:S(2)}) copy-start(bf16[384,768]{1,0:T(8,128)(2,1)} %get-tuple-element.16) | copy-start | bytes 1769476
  325.3 4.7 %copy-start.12 = (bf16[3,768,576]{1,2,0:T(8,128)(2,1)S(1)}, bf16[3,768,576]{1,2,0:T(8,128)(2,1)}, u32[]{:S(2)}) copy-start(bf16[3,768,576]{1,2,0:T(8,128)(2,1)} %get-tuple-element.17) | copy-start | bytes 7962628
  (23 other events, 38.2 us)
Sparse Core Ops, SparseCore 0:
  9.5 15.4 all-gather.4
  26.5 10.4 all-gather.6
  61.5 10.2 reduce-scatter.6
  74.4 9.4 reduce-scatter.4
  104.3 9.7 reduce-scatter.10
  116.8 12.9 reduce-scatter.8
  136.7 188.5 all-reduce.6
where the time goes:
time: 341 us; the launch traced here: 340 us
  waiting for transfers between devices  171 us (50%)
  matrix products  59 us (17%)
  blocking collectives  55.7 us (16%)
  other arithmetic  23.5 us (7%)
  between operations  15.6 us (5%)
  local copies, waits for them, and re-layouts  12.8 us (4%)
    psum x1, waiting for transfers between devices, body(): lax.psum(shares[0].astype(jnp.bfloat16), 'dp').astype(jnp.float32)  141 us
    psum x1, blocking collectives, body(): lax.psum(shares[2].astype(jnp.bfloat16), 'dp').astype(jnp.float32)  44.4 us
    all_gather x1, waiting for transfers between devices, body(): lax.all_gather(qkv_weight, 'tensor', axis=0, tiled=True)  11.1 us
    dot_general x5, matrix products, right_product(): lax.dot_general(left, weight, (((1,), (1,)), ((), ())), preferred_element...  9.54 us
    reduce_scatter x1, waiting for transfers between devices, body(): lax.psum_scatter(right_product(hidden, mlp_weight[2]).astype(jnp.bfloat16...  9.36 us
    reduce_scatter x1, waiting for transfers between devices, body(): lax.psum_scatter(grad_wqkv.astype(jnp.bfloat16), 'tensor', scatter_dimens...  8.69 us
    dot_general x1, matrix products, body(): jnp.einsum('hqk,qhd->khd', probs_b, grad_att, preferred_element_type=f32)  7.95 us
    dot_general x5, matrix products, left_product(): lax.dot_general(left, right, (((0,), (0,)), ((), ())), preferred_element_...  7.5 us
  transfers between devices with their start and end apart: 11, of which 4 were waited for; matrix products, arithmetic and copies ran while one was open for 17% of the time, Pallas kernels for 0%

commit v1 on v0

--- a/solution.py
+++ b/solution.py
@@ -222,7 +222,7 @@
         ).astype(jnp.float32),
     )
     totals = (
-        lax.psum(shares[0].astype(jnp.bfloat16), "dp").astype(jnp.float32),
+        jnp.sum(lax.all_gather(shares[0].astype(jnp.bfloat16), "dp"), axis=0).astype(jnp.float32),
         lax.psum(shares[1].astype(jnp.bfloat16), "dp").astype(jnp.float32),
         lax.psum(shares[2].astype(jnp.bfloat16), "dp").astype(jnp.float32),
         lax.psum(shares[3].astype(jnp.bfloat16), "dp").astype(jnp.float32),

time: 341 us -> 611 us (1.79)
  waiting for transfers between devices: 171 us -> 431 us
  other arithmetic: 23.5 us -> 35.2 us
    all_gather x0 -> x1, waiting for transfers between devices: none -> 295 us  [body(): lax.all_gather(shares[0].astype(jnp.bfloat16), 'dp')]
    psum x1, waiting for transfers between devices: 141 us -> 104 us  [body(): lax.psum(shares[1].astype(jnp.bfloat16), 'dp').astype(jnp.float32)]
    reduce_sum x0 -> x1, other arithmetic: none -> 10.2 us  [body(): jnp.sum(lax.all_gather(shares[0].astype(jnp.bfloat16), 'dp'), axis=0)]
  transfers between devices with their start and end apart: 11 -> 12, of which waited for: 4 -> 5; matrix products, arithmetic and copies ran while one was open for 17% -> 10% of each run, Pallas kernels for 0% -> 0%
where the time goes in v1:
time: 611 us
  waiting for transfers between devices  431 us (71%)
  matrix products  60.3 us (10%)
  blocking collectives  54.8 us (9%)
  other arithmetic  35.2 us (6%)
  between operations  15.5 us (3%)
  local copies, waits for them, and re-layouts  12.1 us (2%)
    all_gather x1, waiting for transfers between devices, body(): lax.all_gather(shares[0].astype(jnp.bfloat16), 'dp')  295 us
    psum x1, waiting for transfers between devices, body(): lax.psum(shares[1].astype(jnp.bfloat16), 'dp').astype(jnp.float32)  104 us
    psum x1, blocking collectives, body(): lax.psum(shares[2].astype(jnp.bfloat16), 'dp').astype(jnp.float32)  43.7 us
  transfers between devices with their start and end apart: 12, of which 5 were waited for; matrix products, arithmetic and copies ran while one was open for 10% of the time, Pallas kernels for 0%

profile of v1, /device:TPU:0, one launch (start us, length us, event | category | flops | bytes accessed | tf_op | source)
XLA Modules:
  0.0 610.6 jit_solution(4019420231046960083)
XLA Ops:
  8.8 2.0 all-gather.1
  11.3 1.8 all-gather.2
  14.0 11.1 %all-gather.7.cloned.1.call-done = bf16[768,2304]{1,0:T(8,128)(2,1)} async-done(((bf16[384,2304]{1,0:T(8,128)(2,1)}), bf16[768,2304]{1,0:T(8,128)(2,1)}) %all-gather.7.cloned.1.call-update) | async-done | bytes 3538960 | tf_op jit(solution)/shard_map/all_gather | solution.py:114
  25.0 3.1 fusion.89
  33.2 2.5 all_gather.29
  38.6 4.9 fusion.71
  43.6 7.0 %fusion.18 = bf16[12,64,256]{2,1,0:T(8,128)(2,1)S(1)} fusion(f32[12,256,512]{2,1,0:T(8,128)} %fusion.71, bf16[256,12,64]{0,2,1:T(8,128)(2,1)S(1)} %bitcast.93, bf16[256,12,64]{0,2,1:T(8,128)(2,1)S(1)} %bitcast.95, pred[]{:T(512)S(6)} %eq.8), kind=kOutput, calls=%fused_computation.29 | convolution fusion | flops 211357184 | bytes 7471105 | tf_op jit(solution)/shard_map/hqk,khd->qhd/dot_general | solution.py:141
  50.6 2.0 fusion.92
  53.4 2.4 all_gather.28
  57.3 2.0 multiply_convert_fusion.1
  61.0 2.0 convolution_add_fusion
  63.0 3.1 convolution_convert_fusion.5
  66.4 7.2 %fusion.1 = f32[12,256,512]{2,1,0:T(8,128)} fusion(bf16[256,12,32]{0,2,1:T(8,128)(2,1)S(1)} %get-tuple-element.31, bf16[256,12,32]{0,2,1:T(8,128)(2,1)S(1)} %get-tuple-element.30, bf16[256,12,64]{0,2,1:T(8,128)(2,1)S(1)} %copy-done.17, bf16[256,12,64]{0,2,1:T(8,128)(2,1)} %bitcast.7, pred[]{:T(512)S(6)} %eq.8), kind=kOutput, calls=%fused_computation.2 | convolution fusion | flops 416026112 | bytes 7471105 | tf_op jit(solution)/shard_map/reduce_sum | solution.py:138
  73.6 2.1 multiply_reduce_fusion
  76.3 9.2 %reduce-scatter.5.cloned.1.call-done = bf16[256,768]{1,0:T(8,128)(2,1)} async-done(((bf16[512,768]{1,0:T(8,128)(2,1)}), bf16[256,768]{1,0:T(8,128)(2,1)}) %reduce-scatter.5.cloned.1.call-update) | async-done | bytes 393232 | tf_op jit(solution)/shard_map/reduce_scatter | solution.py:156
  85.5 2.5 multiply_add_fusion
  90.2 8.0 %fusion.11 = f32[512,12,64]{0,2,1:T(8,128)} fusion(bf16[256,12,64]{0,2,1:T(8,128)(2,1)S(1)} %bitcast.86, f32[12,256,512]{2,1,0:T(8,128)} %fusion.71), kind=kOutput, calls=%fused_computation.18 | convolution fusion | flops 207621632 | bytes 8257536 | tf_op jit(solution)/shard_map/hqk,qhd->khd/dot_general | solution.py:197
  98.3 4.6 multiply_convert_fusion
  108.7 2.2 fusion.17
  113.3 3.1 convolution_convert_fusion
  117.6 1.7 fusion.14
  120.6 1.8 pad_maximum_fusion
  122.5 8.9 %reduce-scatter.9.cloned.1.call-done = bf16[384,2304]{1,0:T(8,128)(2,1)} async-done(((bf16[768,2304]{1,0:T(8,128)(2,1)}), bf16[384,2304]{1,0:T(8,128)(2,1)}) %reduce-scatter.9.cloned.1.call-update) | async-done | bytes 1769488 | tf_op jit(solution)/shard_map/reduce_scatter | solution.py:211
  132.7 3.4 fusion.56
  136.1 2.5 all-reduce.4
  138.8 43.7 %all-reduce.2 = (bf16[384]{0:T(512)(128)(2,1)S(1)}, bf16[384]{0:T(512)(128)(2,1)S(1)}) all-reduce(bf16[384]{0:T(512)(128)(2,1)S(1)} %dynamic-slice.1, bf16[384]{0:T(512)(128)(2,1)S(1)} %dynamic-slice.3), channel_id=1, replica_groups=mesh['dp'=16,'tensor'=2] {'dp'}, use_global_device_ids=true, to_apply=%region_13.14 | all-reduce | flops 768 | bytes 3072 | tf_op jit(solution)/shard_map/psum | solution.py:227
  184.8 104.5 %all-reduce.7.cloned.1.call-done = (bf16[384,768]{1,0:T(8,128)(2,1)}, bf16[3,768,576]{1,2,0:T(8,128)(2,1)}) async-done(((bf16[384,768]{1,0:T(8,128)(2,1)}, bf16[3,768,576]{1,2,0:T(8,128)(2,1)}), (bf16[384,768]{1,0:T(8,128)(2,1)}, bf16[3,768,576]{1,2,0:T(8,128)(2,1)})) %all-reduce.7.cloned.1.call-update) | async-done | bytes 3244048 | tf_op jit(solution)/shard_map/psum | solution.py:226
  289.3 2.2 convert_element_type.171
  291.5 4.6 convert_element_type.174
  296.1 295.5 %all-gather.11.cloned.1.call-done = bf16[6144,2304]{1,0:T(8,128)(2,1)} async-done(((bf16[384,2304]{1,0:T(8,128)(2,1)}), bf16[6144,2304]{1,0:T(8,128)(2,1)}) %all-gather.11.cloned.1.call-update) | async-done | bytes 28311568 | tf_op jit(solution)/shard_map/all_gather | solution.py:225
  591.5 10.2 %reduce_sum.121 = bf16[384,2304]{1,0:T(8,128)(2,1)S(1)} reduce(bf16[16,384,2304]{2,1,0:T(8,128)(2,1)} %bitcast.83, bf16[]{:T(256)} %constant.63.clone.1), dimensions={0}, to_apply=%region_15.16 | reduce | flops 13271040 | bytes 30081026 | tf_op jit(solution)/shard_map/reduce_sum | solution.py:225
  601.7 2.0 convert_element_type.169
  (163 shorter events, 31.4 us)
Async XLA Ops:
  7.2 4.1 copy-start.37
  7.2 17.8 %all-gather.7.cloned.1.call-start = ((), (), s32[]{:S(2)}) async-start(), calls=%async_computation.4 | async-start | bytes 5308416 | tf_op jit(solution)/shard_map/all_gather | solution.py:114
  7.9 42.7 %all-gather.9.cloned.1.call-start = ((), (), s32[]{:S(2)}) async-start(), calls=%async_computation.5 | async-start | bytes 1769472 | tf_op jit(solution)/shard_map/all_gather | solution.py:115
  8.7 65.0 %reduce-scatter.7.cloned.1.call-start = ((), (), s32[]{:S(2)}) async-start(), calls=%async_computation.7 | async-start | bytes 2359296 | tf_op jit(solution)/shard_map/reduce_scatter | solution.py:174
  11.2 17.0 %copy-start.33 = (f32[256]{0:T(256)}, f32[256]{0:T(256)S(1)}, u32[]{:S(2)}) copy-start(f32[256]{0:T(256)S(1)} %add_rsqrt_fusion.1) | copy-start | bytes 3076
  31.8 5.1 copy-start.9
  32.6 4.6 copy-start.25
  32.6 4.6 copy-start.27
  32.6 6.0 copy-start.16
  32.6 6.0 collective-permute-start.1
  32.9 4.4 collective-permute-start
  36.8 6.7 %copy-start.19 = (bf16[256,768]{0,1:T(8,128)(2,1)}, bf16[256,768]{0,1:T(8,128)(2,1)S(1)}, u32[]{:S(2)}) copy-start(bf16[256,768]{0,1:T(8,128)(2,1)S(1)} %copy.30) | copy-start | bytes 1179652
  37.3 29.1 %copy-start.11 = (bf16[256,12,32]{0,2,1:T(8,128)(2,1)}, bf16[256,12,32]{0,2,1:T(8,128)(2,1)S(1)}, u32[]{:S(2)}) copy-start(bf16[256,12,32]{0,2,1:T(8,128)(2,1)S(1)} %get-tuple-element.30) | copy-start | bytes 589828
  37.3 29.1 %copy-start.13 = (bf16[256,12,32]{0,2,1:T(8,128)(2,1)}, bf16[256,12,32]{0,2,1:T(8,128)(2,1)S(1)}, u32[]{:S(2)}) copy-start(bf16[256,12,32]{0,2,1:T(8,128)(2,1)S(1)} %get-tuple-element.31) | copy-start | bytes 589828
  38.6 5.0 copy-start.20
  50.6 5.2 copy-start.10
  63.0 22.5 %reduce-scatter.5.cloned.1.call-start = ((), (), s32[]{:S(2)}) async-start(), calls=%async_computation.6 | async-start | bytes 1179648 | tf_op jit(solution)/shard_map/reduce_scatter | solution.py:156
  66.1 7.5 %copy-start.32 = (f32[256]{0:T(256)S(1)}, f32[256]{0:T(256)}, u32[]{:S(2)}) copy-start(f32[256]{0:T(256)} %copy-done.31) | copy-start | bytes 3076
  66.1 56.3 %reduce-scatter.11.cloned.1.call-start = ((), (), s32[]{:S(2)}) async-start(), calls=%async_computation.9 | async-start | bytes 1769472 | tf_op jit(solution)/shard_map/reduce_scatter | solution.py:214
  90.2 8.0 %copy-start.8 = (bf16[256,768]{0,1:T(8,128)(2,1)}, bf16[256,768]{0,1:T(8,128)(2,1)S(1)}, u32[]{:S(2)}) copy-start(bf16[256,768]{0,1:T(8,128)(2,1)S(1)} %copy.33) | copy-start | bytes 1179652
  98.3 4.6 copy-start.12
  98.3 4.6 copy-start.14
  105.6 5.4 collective-permute-start.2
  105.8 25.6 %reduce-scatter.9.cloned.1.call-start = ((), (), s32[]{:S(2)}) async-start(), calls=%async_computation.8 | async-start | bytes 5308416 | tf_op jit(solution)/shard_map/reduce_scatter | solution.py:211
  107.9 4.2 copy-start.26
  107.9 4.2 copy-start.28
  107.9 4.5 collective-permute-start.3
  116.5 172.9 %all-reduce.7.cloned.1.call-start = ((), (), s32[]{:S(2)}) async-start(), calls=%async_computation.11 | async-start | bytes 6488064 | tf_op jit(solution)/shard_map/psum | solution.py:226
  122.4 9.0 %copy-start.40 = (u32[32]{0:T(128)S(1)}, u32[32]{0:T(128)}, u32[]{:S(2)}) copy-start(u32[32]{0:T(128)} %constant.67) | copy-start | bytes 388
  122.4 10.3 %copy-start.30 = (bf16[256,768]{0,1:T(8,128)(2,1)S(1)}, bf16[256,768]{0,1:T(8,128)(2,1)}, u32[]{:S(2)}) copy-start(bf16[256,768]{0,1:T(8,128)(2,1)} %copy-done.29) | copy-start | bytes 1179652
  122.4 469.1 %all-gather.11.cloned.1.call-start = ((), (), s32[]{:S(2)}) async-start(), calls=%async_computation.10 | async-start | bytes 30081024 | tf_op jit(solution)/shard_map/all_gather | solution.py:225
  132.7 51.0 %copy-start.1 = (f32[256,768]{1,0:T(8,128)S(1)}, f32[256,768]{1,0:T(8,128)}, u32[]{:S(2)}) copy-start(f32[256,768]{1,0:T(8,128)} %copy-done) | copy-start | bytes 2359300
  (21 other events, 41.3 us)
Sparse Core Ops, SparseCore 0:
  9.5 15.4 all-gather.6
  26.5 10.4 all-gather.8
  63.1 10.2 reduce-scatter.6
  76.0 9.4 reduce-scatter.4
  105.9 9.7 reduce-scatter.10
  118.4 12.9 reduce-scatter.8
  137.8 151.5 all-reduce.6
  292.1 299.3 all-gather.10
